TPU v7x, 32 devices: a whole 2x2x4 slice. The times are simulated.
32 devices in a mesh: group: 2 (over y), context: 4 (over z), head: 4 (over x, core).
Axes of the slice: x: 2, y: 2, z: 4, core: 2. Of those that a mesh axis runs over, the one named last changes fastest.
Arguments:
- dn_query: bfloat16 [1024, 2048], P(('group', 'context'), 'head'), parts along dimension 0, may hold values from -6 to 6
- dn_key: bfloat16 [1024, 2048], P(('group', 'context'), 'head'), parts along dimension 0, may hold values from -6 to 6
- dn_value: bfloat16 [1024, 4096], P(('group', 'context'), 'head'), parts along dimension 0, may hold values from -6 to 6
- dn_gate: bfloat16 [1024, 4096], P(('group', 'context'), 'head'), parts along dimension 0, may hold values from -6 to 6
- dn_beta_logit: float32 [1024, 32], P(('group', 'context'), 'head'), parts along dimension 0, may hold values from -6 to 6
- dn_decay: float32 [1024, 32], P(('group', 'context'), 'head'), parts along dimension 0, may hold values from -1 to 0
- dn_norm_gain: float32 [128], replicated, may hold values from 0.1 to 1.9
- prefix_state: bfloat16 [4, 32, 128, 128], P('group', 'head', 'context'), parts along dimension 0, may hold values from -6 to 6
- at_query: bfloat16 [1024, 4096], P(('group', 'context'), 'head'), parts along dimension 0, may hold values from -6 to 6
- at_gate: bfloat16 [1024, 4096], P(('group', 'context'), 'head'), parts along dimension 0, may hold values from -6 to 6
- at_key: bfloat16 [1024, 512], P(('group', 'context')), parts along dimension 0, may hold values from -6 to 6
- at_value: bfloat16 [1024, 512], P(('group', 'context')), parts along dimension 0, may hold values from -6 to 6
- prefix_key: bfloat16 [16, 64, 512], P(('group', 'context')), parts along dimension 0, may hold values from -6 to 6
- prefix_value: bfloat16 [16, 64, 512], P(('group', 'context')), parts along dimension 0, may hold values from -6 to 6
- req_len: int32 [8], P('group'), parts along dimension 0, may hold values from 1 to 256, 512 in all
- req_prefix: int32 [8], P('group'), parts along dimension 0, may hold values from 0 to 1, as said below
- req_offset: int32 [8], P('group'), parts along dimension 0, may hold values from 64 to 256, as said below
- block_table: int32 [16], P('group'), parts along dimension 0, may hold values from 0 to 7, each once
Outputs:
- dn_out: bfloat16 [1024, 4096], P(('group', 'context'), 'head'), parts along dimension 0
- at_out: bfloat16 [1024, 4096], P(('group', 'context'), 'head'), parts along dimension 0
There are 2 independent parts, one for each index of `group`. A program takes and returns all parts, laid end to end along the dimension named above; an argument that names none is the same for every part. Nothing has to cross between parts.
Inputs may be any that keep to these rules, and one draw needn't show every extreme that they name: `req_len`: requests lie one after another in row order; the longest has exactly 256 new tokens. `req_prefix`: every prefix is extended by one or more requests. `req_offset`: equal for the requests of one prefix: the number of its cached positions; one prefix holds 256, another from a quarter to a half of 256. `block_table`: entry p * 4 + j is the slot of block j of prefix p; every slot once.
All inputs are finite; a program needn't handle non-finite values.
Results may differ from a plain program's by a relative error of at most 0.011.
Values may be sent and summed in bfloat16 or wider, within the bound.
A program may use at most 128 MiB of HBM per device.

v0:
```python
import math
import jax
import jax.numpy as jnp
from jax import lax
from jax.sharding import PartitionSpec as P

VH = 32
KH = 16
DK = 128
DV = 128
HQ = 16
KVH = 2
HD = 256
ROT = 64
ROPE_THETA = 10000000.0
YARN_FACTOR = 4.0
YARN_ANCHOR = 262144.0
NEG_LARGE = -1e30
HIGH = lax.Precision.HIGHEST


def carried_in(x, axis, join, neutral):
    place = lax.axis_index(axis)
    gathered = jax.tree.map(
        lambda a, kind: lax.all_gather(a.astype(kind), axis),
        x,
        (jnp.bfloat16, jnp.bfloat16, jnp.bfloat16),
    )
    state = jax.tree.map(lambda a, e: jnp.zeros_like(a) + jnp.asarray(e, a.dtype), x, neutral)

    def one(turn, state):
        return join(
            state,
            jax.tree.map(
                lambda a, own: lax.dynamic_index_in_dim(a, turn, 0, False).astype(own.dtype),
                gathered,
                x,
            ),
        )

    return lax.fori_loop(0, place, one, state)


def yarn_tables(positions, rotary):
    half = rotary // 2
    log_theta = math.log(ROPE_THETA)
    lower = max(
        math.floor(rotary * math.log(YARN_ANCHOR / (64.0 * math.pi)) / (2.0 * log_theta)), 0
    )
    upper = min(
        math.ceil(rotary * math.log(YARN_ANCHOR / (2.0 * math.pi)) / (2.0 * log_theta)), rotary - 1
    )
    spread = float(upper - lower)
    index = jnp.arange(half, dtype=jnp.float32)
    plain_frequency = jnp.exp(index * (-2.0 * log_theta / rotary))
    keep = 1.0 - jnp.clip((index - lower) / spread, 0.0, 1.0)
    frequency = plain_frequency * keep + plain_frequency / YARN_FACTOR * (1.0 - keep)
    angles = positions.astype(jnp.float32)[:, None] * frequency[None, :]
    attention_factor = 0.1 * math.log(YARN_FACTOR) + 1.0
    return (jnp.cos(angles) * attention_factor, jnp.sin(angles) * attention_factor)


def rotate(values, cosines, sines, rotary):
    half = rotary // 2
    first = values[..., :half]
    second = values[..., half:rotary]
    cosines = cosines[:, None, :]
    sines = sines[:, None, :]
    return jnp.concatenate(
        [first * cosines - second * sines, second * cosines + first * sines, values[..., rotary:]],
        axis=-1,
    )


def unit_rows(values):
    return values * lax.rsqrt(jnp.sum(values * values, axis=-1, keepdims=True) + 1e-06)


def row_layout(rows, req_len, req_prefix, req_offset):
    starts = jnp.cumsum(req_len) - req_len
    leading_found = (starts[None, :] <= rows[:, None]).astype(jnp.int32)
    segment = jnp.sum(leading_found, axis=1) - 1
    choose = (segment[:, None] == jnp.arange(req_len.shape[0], dtype=jnp.int32)[None, :]).astype(
        jnp.int32
    )
    first = jnp.sum(choose * starts[None, :], axis=1)
    prefix = jnp.sum(choose * req_prefix[None, :], axis=1)
    offset = jnp.sum(choose * req_offset[None, :], axis=1)
    return (segment, first, prefix, offset, offset + rows - first)


def absorb(state, queries, search_handles, values, visible):
    peak, total, summed = state
    scores = jnp.einsum(
        "thd,nd->thn", queries, search_handles, preferred_element_type=jnp.float32
    ) * search_handles.shape[-1] ** (-0.5)
    seen = visible[:, None, :]
    scores = jnp.where(seen, scores, NEG_LARGE)
    new_peak = jnp.maximum(peak, jnp.max(scores, axis=-1))
    weights = jnp.where(seen, jnp.exp(scores - new_peak[..., None]), 0.0)
    shrink = jnp.exp(peak - new_peak)
    total = total * shrink + jnp.sum(weights, axis=-1)
    summed = summed * shrink[..., None] + jnp.einsum(
        "thn,nd->thd", weights.astype(jnp.bfloat16), values, preferred_element_type=jnp.float32
    )
    return (new_peak, total, summed)


def compose(earlier, later):
    map_early, add_early, flag_early = earlier
    map_late, add_late, flag_late = later
    fresh = flag_late > 0.5
    joined_map = jnp.where(
        fresh, map_late, jnp.einsum("hij,hjk->hik", map_early, map_late, precision=HIGH)
    )
    joined_add = jnp.where(
        fresh, add_late, jnp.einsum("hvj,hjk->hvk", add_early, map_late, precision=HIGH) + add_late
    )
    return (joined_map, joined_add, jnp.maximum(flag_early, flag_late))


def shards(
    dn_query,
    dn_key,
    dn_value,
    dn_gate,
    dn_beta_logit,
    dn_decay,
    dn_norm_gain,
    prefix_state,
    at_query,
    at_gate,
    at_key,
    at_value,
    prefix_key,
    prefix_value,
    req_len,
    req_prefix,
    req_offset,
    block_table,
):
    tokens_here = dn_query.shape[0]
    key_heads = dn_query.shape[1] // DK
    value_heads = dn_value.shape[1] // DV
    query_heads = at_query.shape[1] // HD
    device = lax.axis_index("context")
    row_start = device * tokens_here
    rows = row_start + jnp.arange(tokens_here, dtype=jnp.int32)
    segment, first, prefix, offset, position = row_layout(rows, req_len, req_prefix, req_offset)
    query = jnp.repeat(
        unit_rows(dn_query.reshape(tokens_here, key_heads, DK).astype(jnp.float32)) * DK ** (-0.5),
        VH // KH,
        axis=1,
    )
    key = jnp.repeat(
        unit_rows(dn_key.reshape(tokens_here, key_heads, DK).astype(jnp.float32)), VH // KH, axis=1
    )
    query_heads_first = jnp.transpose(query, (1, 0, 2))
    key_heads_first = jnp.transpose(key, (1, 0, 2))
    value_heads_first = jnp.transpose(
        dn_value.reshape(tokens_here, value_heads, DV).astype(jnp.float32), (1, 0, 2)
    )
    beta = jax.nn.sigmoid(dn_beta_logit).T
    same = segment[:, None] == segment[None, :]
    causal = same & (rows[:, None] >= rows[None, :])
    strict = same & (rows[:, None] > rows[None, :])
    running = jnp.dot(causal.astype(jnp.float32), dn_decay, precision=HIGH).T
    gaps = running[:, :, None] - running[:, None, :]
    decay_mat = jnp.where(causal[None], jnp.exp(jnp.where(causal[None], gaps, 0.0)), 0.0)
    key_gram = jnp.einsum("hid,hjd->hij", key_heads_first, key_heads_first, precision=HIGH)
    query_key = jnp.einsum("hid,hjd->hij", query_heads_first, key_heads_first, precision=HIGH)
    lower_mat = jnp.where(strict[None], beta[:, :, None] * key_gram * decay_mat, 0.0)
    system = jnp.eye(tokens_here, dtype=jnp.float32)[None] + lower_mat
    start_decay = jnp.exp(running)
    solve_values = beta[:, :, None] * value_heads_first
    solve_keys = (beta * start_decay)[:, :, None] * key_heads_first
    solved = jax.scipy.linalg.solve_triangular(
        system, jnp.concatenate([solve_values, solve_keys], axis=2), lower=True, unit_diagonal=True
    )
    update = solved[:, :, :DV]
    wy_keys = solved[:, :, DV:]
    mixing = decay_mat * query_key
    local_out = jnp.einsum("hij,hjv->hiv", mixing, update, precision=HIGH)
    reach = start_decay[:, :, None] * query_heads_first - jnp.einsum(
        "hij,hjk->hik", mixing, wy_keys, precision=HIGH
    )
    tail = segment == segment[tokens_here - 1]
    end_gaps = running[:, tokens_here - 1 : tokens_here] - running
    end_weight = jnp.where(tail[None, :], jnp.exp(jnp.where(tail[None, :], end_gaps, 0.0)), 0.0)
    end_decay = start_decay[:, tokens_here - 1]
    identity_mat = jnp.eye(DK, dtype=jnp.float32)
    carry_map = end_decay[:, None, None] * identity_mat[None] - jnp.einsum(
        "hjk,hj,hjl->hkl", wy_keys, end_weight, key_heads_first, precision=HIGH
    )
    carry_add = jnp.einsum("hjv,hj,hjl->hvl", update, end_weight, key_heads_first, precision=HIGH)
    restart = (first[tokens_here - 1] >= row_start).astype(jnp.float32)
    identity = (
        jnp.broadcast_to(identity_mat, (value_heads, DK, DK)),
        jnp.zeros((value_heads, DV, DK), jnp.float32),
        jnp.zeros((), jnp.float32),
    )
    into_map, into_add, into_flag = carried_in(
        (carry_map, carry_add, restart), "context", compose, identity
    )
    carried = ((segment == segment[0]) & (first[0] < row_start))[None, :, None]
    through = jnp.einsum("hkl,hil->hik", into_map, reach, precision=HIGH)
    extra = jnp.einsum("hvk,hik->hiv", into_add, reach, precision=HIGH)
    weight_vec = jnp.where(carried, through, reach).astype(jnp.bfloat16)
    core = local_out + jnp.where(carried, extra, 0.0)
    owner_ids = jnp.arange(prefix_state.shape[0], dtype=jnp.int32)
    select = (prefix[None, :] == owner_ids[:, None]).astype(jnp.bfloat16)
    masked = select[:, None, :, None] * weight_vec[None]
    state_part = jnp.einsum(
        "phik,phvk->hiv",
        masked,
        lax.all_gather(prefix_state, "context", axis=2, tiled=True),
        preferred_element_type=jnp.float32,
    )
    core = core + state_part
    core_rows = jnp.transpose(core, (1, 0, 2))
    normed = core_rows * lax.rsqrt(jnp.mean(core_rows * core_rows, axis=-1, keepdims=True) + 1e-06)
    gate_rows = dn_gate.reshape(tokens_here, value_heads, DV).astype(jnp.float32)
    dn_out = (
        (normed * dn_norm_gain * jax.nn.silu(gate_rows))
        .reshape(tokens_here, value_heads * DV)
        .astype(jnp.bfloat16)
    )
    group = HQ // KVH
    kv_head = lax.axis_index("head") * query_heads // group
    cosines, sines = yarn_tables(position, ROT)
    query_rot = rotate(
        at_query.reshape(tokens_here, query_heads, HD).astype(jnp.float32), cosines, sines, ROT
    ).astype(jnp.bfloat16)
    new_key = lax.dynamic_slice_in_dim(at_key, kv_head * HD, HD, 1).reshape(tokens_here, 1, HD)
    new_key = (
        rotate(new_key.astype(jnp.float32), cosines, sines, ROT)
        .reshape(tokens_here, HD)
        .astype(jnp.bfloat16)
    )
    new_value = lax.dynamic_slice_in_dim(at_value, kv_head * HD, HD, 1)
    cached_key = lax.dynamic_slice_in_dim(prefix_key, kv_head * HD, HD, 2)
    cached_value = lax.dynamic_slice_in_dim(prefix_value, kv_head * HD, HD, 2)
    table_index = jnp.arange(block_table.shape[0], dtype=jnp.int32)
    blocks_per_prefix = block_table.shape[0] // prefix_state.shape[0]
    state = (
        jnp.full((tokens_here, query_heads), NEG_LARGE, jnp.float32),
        jnp.zeros((tokens_here, query_heads), jnp.float32),
        jnp.zeros((tokens_here, query_heads, HD), jnp.float32),
    )
    search_handles = lax.all_gather(cached_key, "context", axis=0, tiled=True)
    values = lax.all_gather(cached_value, "context", axis=0, tiled=True)
    count = search_handles.shape[0]
    width = search_handles.shape[1]
    slots = jnp.arange(count, dtype=jnp.int32)
    entry = jnp.sum(
        jnp.where(block_table[None, :] == slots[:, None], table_index[None, :], 0), axis=1
    )
    owner = jnp.repeat(entry // blocks_per_prefix, width)
    where_in = (
        (entry % blocks_per_prefix)[:, None] * width + jnp.arange(width, dtype=jnp.int32)[None, :]
    ).reshape(count * width)
    visible = (owner[None, :] == prefix[:, None]) & (where_in[None, :] < offset[:, None])
    flat_keys = search_handles.reshape(count * width, search_handles.shape[2])
    flat_values = values.reshape(count * width, values.shape[2])
    state = absorb(state, query_rot, flat_keys, flat_values, visible)
    search_handles = lax.all_gather(new_key, "context", axis=0, tiled=True)
    values = lax.all_gather(new_value, "context", axis=0, tiled=True)
    key_rows = jnp.arange(search_handles.shape[0], dtype=jnp.int32)
    key_segment = row_layout(key_rows, req_len, req_prefix, req_offset)[0]
    visible = (key_segment[None, :] == segment[:, None]) & (key_rows[None, :] <= rows[:, None])
    state = absorb(state, query_rot, search_handles, values, visible)
    peak, total, summed = state
    attention = summed / total[..., None]
    gate_att = at_gate.reshape(tokens_here, query_heads, HD).astype(jnp.float32)
    at_out = (
        (attention * jax.nn.sigmoid(gate_att))
        .reshape(tokens_here, query_heads * HD)
        .astype(jnp.bfloat16)
    )
    return (dn_out, at_out)


def solution(mesh):
    placed = (
        P(("group", "context"), "head"),
        P(("group", "context"), "head"),
        P(("group", "context"), "head"),
        P(("group", "context"), "head"),
        P(("group", "context"), "head"),
        P(("group", "context"), "head"),
        P(),
        P("group", "head", "context", None),
        P(("group", "context"), "head"),
        P(("group", "context"), "head"),
        P(("group", "context"), None),
        P(("group", "context"), None),
        P(("group", "context"), None, None),
        P(("group", "context"), None, None),
        P("group"),
        P("group"),
        P("group"),
        P("group"),
    )
    return jax.shard_map(
        shards,
        mesh=mesh,
        in_specs=placed,
        out_specs=(P(("group", "context"), "head"), P(("group", "context"), "head")),
        check_vma=False,
    )
```

profile of v0, /device:TPU:26, one launch (start us, length us, event | category | flops | bytes accessed | tf_op | source)
XLA Modules:
  0.0 243.3 jit_solution(15976261732324481945)
XLA Ops:
  12.8 2.1 fusion.15
  14.9 79.4 %custom-call.4 = f32[8,1,128,128]{2,3,1,0:T(8,128)S(1)} custom-call(f32[8,1,128,128]{3,2,1,0:T(8,128)} %fusion.15), custom_call_target="InvertDiagBlocksLowerTriangular" | custom-call | tf_op jit(solution)/shard_map/jit(_solve_triangular)/vmap()/triangular_solve | solution.py:177
  94.3 1.8 compare_and_fusion.3
  96.7 1.0 fusion.22
  97.8 1.7 convolution_convert_fusion
  99.8 1.7 fusion.20
  104.2 16.7 %all-gather.2 = bf16[512,1,256]{0,2,1:T(8,128)(2,1)} all-gather(bf16[128,1,256]{0,2,1:T(8,128)(2,1)S(1)} %pad_maximum_fusion.1), channel_id=4, replica_groups=mesh['group'=2,'context'=4,'head'=4] {'context'}, dimensions={0}, use_global_device_ids=true | all-gather | bytes 327680 | tf_op jit(solution)/shard_map/all_gather | solution.py:266
  121.9 16.6 %all_gather.40 = bf16[8,64,256]{2,1,0:T(8,128)(2,1)} all-gather(bf16[2,64,256]{2,1,0:T(8,128)(2,1)S(1)} %constant_dynamic-slice_fusion.3), channel_id=1, replica_groups=mesh['group'=2,'context'=4,'head'=4] {'context'}, dimensions={0}, use_global_device_ids=true | all-gather | bytes 327680 | tf_op jit(solution)/shard_map/all_gather | solution.py:250
  138.9 16.8 %all_gather.41 = bf16[8,64,256]{2,1,0:T(8,128)(2,1)} all-gather(bf16[2,64,256]{2,1,0:T(8,128)(2,1)S(1)} %constant_dynamic-slice_fusion.2), channel_id=1, replica_groups=mesh['group'=2,'context'=4,'head'=4] {'context'}, dimensions={0}, use_global_device_ids=true | all-gather | bytes 327680 | tf_op jit(solution)/shard_map/all_gather | solution.py:251
  155.7 16.5 %all_gather.43 = bf16[512,256]{1,0:T(8,128)(2,1)} all-gather(bf16[128,256]{1,0:T(8,128)(2,1)S(1)} %constant_dynamic-slice_fusion.4), channel_id=1, replica_groups=mesh['group'=2,'context'=4,'head'=4] {'context'}, dimensions={0}, use_global_device_ids=true | all-gather | bytes 327680 | tf_op jit(solution)/shard_map/all_gather | solution.py:267
  172.5 1.0 copy.164
  180.1 1.2 fusion.18
  181.8 1.9 dynamic-update-slice
  183.7 2.3 fusion.19
  186.6 8.6 %all-reduce = bf16[4]{0:T(256)(128)(2,1)} all-reduce(bf16[4]{0:T(256)(128)(2,1)S(1)} %copy-done.39), channel_id=1, replica_groups=mesh['group'=2,'context'=4,'head'=4] {'context'}, use_global_device_ids=true, to_apply=%add | all-reduce | flops 4 | bytes 16
  195.3 1.1 copy.165
  198.4 0.9 copy-done.13
  199.7 15.1 %all_gather.39 = bf16[2,8,128,128]{3,2,0,1:T(8,128)(2,1)S(1)} all-gather(bf16[2,8,32,128]{3,2,0,1:T(8,128)(2,1)S(1)} %copy.150), channel_id=1, replica_groups=mesh['group'=2,'context'=4,'head'=4] {'context'}, dimensions={2}, use_global_device_ids=true | all-gather | bytes 655360 | tf_op jit(solution)/shard_map/all_gather | solution.py:216
  216.1 1.2 convolution_multiply_fusion.3
  217.3 1.5 fusion.43
  220.2 11.2 %while.14 = (s32[]{:T(128)}, f32[8,128,128]{1,2,0:T(8,128)S(1)}, f32[8,128,128]{1,2,0:T(8,128)S(1)}, s32[]{:T(128)}, bf16[4]{0:T(256)(128)(2,1)S(1)}, /*index=5*...) while((s32[]{:T(128)}, f32[8,128,128]{1,2,0:T(8,128)S(1)}, ...), condition=%wide.region_6.7_spmd, body=%wide.region_5.6_spmd.sunk | while | flops 403308544 | bytes 7340196 | solution.py:41
  220.2 1.1 constant_dynamic-slice_fusion.7
  223.9 1.1 constant_dynamic-slice_fusion.7
  227.7 1.1 constant_dynamic-slice_fusion.7
  (191 shorter events, 32.6 us)
Async XLA Ops:
  7.2 96.5 %copy-start = (bf16[128,512]{1,0:T(8,128)(2,1)S(1)}, bf16[128,512]{1,0:T(8,128)(2,1)}, u32[]{:S(2)}) copy-start(bf16[128,512]{1,0:T(8,128)(2,1)} %param.30) | copy-start | bytes 393220
  7.2 212.3 %all-gather.8.cloned.1.call-start = ((), (), s32[]{:S(2)}) async-start(), calls=%async_computation.1 | async-start | bytes 1310720 | tf_op jit(solution)/shard_map/all_gather | solution.py:25
  7.2 3.6 %copy-start.15 = (bf16[128,512]{1,0:T(8,128)(2,1)S(1)}, bf16[128,512]{1,0:T(8,128)(2,1)}, u32[]{:S(2)}) copy-start(bf16[128,512]{1,0:T(8,128)(2,1)} %param.21) | copy-start | bytes 393220
  7.3 92.5 %copy-start.2 = (f32[128,128]{1,0:T(8,128)}, f32[128,128]{1,0:T(8,128)S(1)}, u32[]{:S(2)}) copy-start(f32[128,128]{1,0:T(8,128)S(1)} %get-tuple-element.158) | copy-start | bytes 196612
  9.0 166.3 %copy-start.28 = (s32[128]{0:T(128)}, s32[128]{0:T(128)S(1)}, u32[]{:S(2)}) copy-start(s32[128]{0:T(128)S(1)} %get-tuple-element.108) | copy-start | bytes 1540
  9.0 1.3 copy-start.34
  10.6 85.6 %copy-start.18 = (f32[8,128]{1,0:T(8,128)}, f32[8,128]{1,0:T(8,128)S(1)}, u32[]{:S(2)}) copy-start(f32[8,128]{1,0:T(8,128)S(1)} %convolution_bitcast_fusion.3) | copy-start | bytes 12292
  11.4 1.0 copy-start.10
  96.2 3.4 %copy-start.20 = (f32[8,128]{1,0:T(8,128)}, f32[8,128]{1,0:T(8,128)S(1)}, u32[]{:S(2)}) copy-start(f32[8,128]{1,0:T(8,128)S(1)} %get-tuple-element.135) | copy-start | bytes 12292
  99.5 120.0 %all-gather.6.cloned.1.call-start = ((), (), s32[]{:S(2)}) async-start(), calls=%async_computation | async-start | bytes 1310720 | tf_op jit(solution)/shard_map/all_gather | solution.py:25
  120.9 1.0 copy-start.22
  121.9 16.6 %copy-start.36 = (s32[8]{0:T(128)S(1)}, s32[8]{0:T(128)}, u32[]{:S(2)}) copy-start(s32[8]{0:T(128)} %param.37) | copy-start | bytes 100
  121.9 17.0 %copy-start.23 = (bf16[2,64,512]{2,1,0:T(8,128)(2,1)S(1)}, bf16[2,64,512]{2,1,0:T(8,128)(2,1)}, u32[]{:S(2)}) copy-start(bf16[2,64,512]{2,1,0:T(8,128)(2,1)} %param.33) | copy-start | bytes 393220
  138.9 16.8 %copy-start.24 = (bf16[128,512]{1,0:T(8,128)(2,1)S(1)}, bf16[128,512]{1,0:T(8,128)(2,1)}, u32[]{:S(2)}) copy-start(bf16[128,512]{1,0:T(8,128)(2,1)} %param.31) | copy-start | bytes 393220
  155.7 16.5 %copy-start.12 = (bf16[128,1024]{1,0:T(8,128)(2,1)S(1)}, bf16[128,1024]{1,0:T(8,128)(2,1)}, u32[]{:S(2)}) copy-start(bf16[128,1024]{1,0:T(8,128)(2,1)} %param.29) | copy-start | bytes 786436
  172.5 1.0 copy-start.16
  175.2 1.0 copy-start.14
  178.2 1.9 copy-start.6
  180.1 3.6 %copy-start.4 = (f32[128,4,256]{2,0,1:T(8,128)S(1)}, f32[128,4,256]{2,0,1:T(8,128)}, u32[]{:S(2)}) copy-start(f32[128,4,256]{2,0,1:T(8,128)} %copy.164) | copy-start | bytes 1572868
  183.7 2.3 copy-start.9
  186.0 9.2 %copy-start.3 = (f32[128,128]{1,0:T(8,128)S(1)}, f32[128,128]{1,0:T(8,128)}, u32[]{:S(2)}) copy-start(f32[128,128]{1,0:T(8,128)} %copy-done.2) | copy-start | bytes 196612
  199.7 15.2 %copy-start.29 = (s32[128]{0:T(128)S(1)}, s32[128]{0:T(128)}, u32[]{:S(2)}) copy-start(s32[128]{0:T(128)} %copy-done.28) | copy-start | bytes 1540
  217.3 1.5 copy-start.21
  232.7 1.0 copy-start.1
  (18 other events, 13.3 us)
Sparse Core Ops, SparseCore 0:
  99.7 32.8 all-gather.7
  134.7 33.2 all-gather.5
where the time goes:
time: 244 us; the launch traced here: 243 us
  blocking collectives  90.3 us (37%)
  other arithmetic  87.6 us (36%)
  local copies, waits for them, and re-layouts  27.8 us (11%)
  matrix products  19.2 us (8%)
  between operations  16.1 us (7%)
    another operation x2, other arithmetic, shards(): jax.scipy.linalg.solve_triangular(system, jnp.concatenate([solve_values,...  79.4 us
    all_gather x1, blocking collectives, shards(): values = lax.all_gather(cached_value, 'context', axis=0, tiled=True)  16.8 us
    all_gather x1, blocking collectives, shards(): search_handles = lax.all_gather(new_key, 'context', axis=0, tiled=True)  16.7 us
    all_gather x1, blocking collectives, shards(): search_handles = lax.all_gather(cached_key, 'context', axis=0, tiled=True)  16.6 us
    all_gather x1, blocking collectives, shards(): values = lax.all_gather(new_value, 'context', axis=0, tiled=True)  16.5 us
    unnamed x91, local copies, waits for them, and re-layouts  15.3 us
    all_gather x1, blocking collectives, shards(): lax.all_gather(prefix_state, 'context', axis=2, tiled=True)  15.1 us
    unnamed x1, blocking collectives  8.58 us
  transfers between devices with their start and end apart: 2, of which 0 were waited for; matrix products, arithmetic and copies ran while one was open for 9% of the time, Pallas kernels for 0%

commit v1 on v0

--- a/solution.py
+++ b/solution.py
@@ -264,7 +264,16 @@
     flat_values = values.reshape(count * width, values.shape[2])
     state = absorb(state, query_rot, flat_keys, flat_values, visible)
     search_handles = lax.all_gather(new_key, "context", axis=0, tiled=True)
-    values = lax.all_gather(new_value, "context", axis=0, tiled=True)
+    ways = lax.axis_size("context")
+    up = [(d, (d + 1) % ways) for d in range(ways)]
+    down = [(d, (d - 1) % ways) for d in range(ways)]
+    earlier_2, later_2 = ([new_value], [new_value])
+    for _ in range(ways // 2):
+        earlier_2.append(lax.ppermute(earlier_2[-1], "context", up))
+    for _ in range((ways - 1) // 2):
+        later_2.append(lax.ppermute(later_2[-1], "context", down))
+    line = jnp.concatenate([*earlier_2[::-1], *later_2[1:]], axis=0)
+    values = jnp.roll(line, (lax.axis_index("context") - ways // 2) * new_value.shape[0], axis=0)
     key_rows = jnp.arange(search_handles.shape[0], dtype=jnp.int32)
     key_segment = row_layout(key_rows, req_len, req_prefix, req_offset)[0]
     visible = (key_segment[None, :] == segment[:, None]) & (key_rows[None, :] <= rows[:, None])

time: 244 us -> 227 us (0.930)
  blocking collectives: 90.3 us -> 72.5 us
  starting transfers between devices: 0.08 us -> 3.99 us
  other arithmetic: 87.6 us -> 83.9 us
  local copies, waits for them, and re-layouts: 27.8 us -> 30.6 us
    all_gather x1 -> x0, blocking collectives: 16.5 us -> none  [shards(): values = lax.all_gather(new_value, 'context', axis=0, tiled=True)]
    ppermute x0 -> x3, starting transfers between devices: none -> 3.91 us  [the longest x2 2.11 us: shards(): earlier_2.append(lax.ppermute(earlier_2[-1], 'context', up))]
    unnamed x91 -> x74, local copies, waits for them, and re-layouts: 15.3 us -> 17.5 us
  transfers between devices with their start and end apart: 2 -> 5, of which waited for: 0 -> 0; matrix products, arithmetic and copies ran while one was open for 9% -> 11% of each run, Pallas kernels for 0% -> 0%
where the time goes in v1:
time: 227 us; the launch traced here: 226 us
  other arithmetic  83.9 us (37%)
  blocking collectives  72.5 us (32%)
  local copies, waits for them, and re-layouts  30.6 us (13%)
  matrix products  17.2 us (8%)
  between operations  16 us (7%)
  starting transfers between devices  3.99 us (2%)
    another operation x2, other arithmetic, shards(): jax.scipy.linalg.solve_triangular(system, jnp.concatenate([solve_values,...  78.6 us
    unnamed x74, local copies, waits for them, and re-layouts  17.5 us
    all_gather x1, blocking collectives, shards(): values = lax.all_gather(cached_value, 'context', axis=0, tiled=True)  16.7 us
    all_gather x1, blocking collectives, shards(): search_handles = lax.all_gather(new_key, 'context', axis=0, tiled=True)  16.7 us
    all_gather x1, blocking collectives, shards(): search_handles = lax.all_gather(cached_key, 'context', axis=0, tiled=True)  15.6 us
    all_gather x1, blocking collectives, shards(): lax.all_gather(prefix_state, 'context', axis=2, tiled=True)  14.8 us
    unnamed x1, blocking collectives  8.62 us
    dynamic_slice x12, local copies, waits for them, and re-layouts, one(): lax.dynamic_index_in_dim(a, turn, 0, False).astype(own.dtype)  6.04 us
  transfers between devices with their start and end apart: 5, of which 0 were waited for; matrix products, arithmetic and copies ran while one was open for 11% of the time, Pallas kernels for 0%

profile of v1, /device:TPU:26, one launch (start us, length us, event | category | flops | bytes accessed | tf_op | source)
XLA Modules:
  0.0 226.3 jit_solution(2586210909350464604)
XLA Ops:
  12.7 1.3 fusion.15
  14.0 78.6 %custom-call.4 = f32[8,1,128,128]{2,3,1,0:T(8,128)S(1)} custom-call(f32[8,1,128,128]{3,2,1,0:T(8,128)S(1)} %fusion.15), custom_call_target="InvertDiagBlocksLowerTriangular" | custom-call | tf_op jit(solution)/shard_map/jit(_solve_triangular)/vmap()/triangular_solve | solution.py:177
  92.6 1.3 compare_and_fusion.3
  94.5 1.0 fusion.22
  95.5 1.7 convolution_convert_fusion
  99.0 1.8 collective-permute-start.2
  101.0 1.7 fusion.20
  105.6 1.2 convolution_multiply_fusion.3
  106.8 1.5 fusion.43
  109.4 16.7 %all-gather.2 = bf16[512,1,256]{0,2,1:T(8,128)(2,1)S(1)} all-gather(bf16[128,1,256]{0,2,1:T(8,128)(2,1)S(1)} %pad_maximum_fusion.1), channel_id=4, replica_groups=mesh['group'=2,'context'=4,'head'=4] {'context'}, dimensions={0}, use_global_device_ids=true | all-gather | bytes 327680 | tf_op jit(solution)/shard_map/all_gather | solution.py:266
  127.0 15.6 %all_gather.37 = bf16[8,64,256]{2,1,0:T(8,128)(2,1)} all-gather(bf16[2,64,256]{2,1,0:T(8,128)(2,1)S(1)} %constant_dynamic-slice_fusion.5), channel_id=1, replica_groups=mesh['group'=2,'context'=4,'head'=4] {'context'}, dimensions={0}, use_global_device_ids=true | all-gather | bytes 327680 | tf_op jit(solution)/shard_map/all_gather | solution.py:250
  143.1 16.7 %all_gather.38 = bf16[8,64,256]{2,1,0:T(8,128)(2,1)} all-gather(bf16[2,64,256]{2,1,0:T(8,128)(2,1)S(1)} %constant_dynamic-slice_fusion.4), channel_id=1, replica_groups=mesh['group'=2,'context'=4,'head'=4] {'context'}, dimensions={0}, use_global_device_ids=true | all-gather | bytes 327680 | tf_op jit(solution)/shard_map/all_gather | solution.py:251
  163.5 1.2 fusion.18
  167.2 1.9 collective-permute-start.1
  169.1 14.8 %all_gather.36 = bf16[2,8,128,128]{3,2,0,1:T(8,128)(2,1)S(1)} all-gather(bf16[2,8,32,128]{3,2,0,1:T(8,128)(2,1)S(1)} %copy.150), channel_id=1, replica_groups=mesh['group'=2,'context'=4,'head'=4] {'context'}, dimensions={2}, use_global_device_ids=true | all-gather | bytes 655360 | tf_op jit(solution)/shard_map/all_gather | solution.py:216
  183.9 8.6 %all-reduce = bf16[4]{0:T(256)(128)(2,1)} all-reduce(bf16[4]{0:T(256)(128)(2,1)S(1)} %dynamic-update-slice), channel_id=1, replica_groups=mesh['group'=2,'context'=4,'head'=4] {'context'}, use_global_device_ids=true, to_apply=%add | all-reduce | flops 4 | bytes 16
  193.5 1.1 copy.152
  194.8 0.9 constant_dynamic-update-slice_fusion.7
  200.0 1.1 fusion.19
  201.1 1.1 copy.165
  203.8 11.3 %while.14 = (s32[]{:T(128)}, f32[8,128,128]{1,2,0:T(8,128)S(1)}, f32[8,128,128]{1,2,0:T(8,128)S(1)}, s32[]{:T(128)}, bf16[4]{0:T(256)(128)(2,1)S(1)}, /*index=5*...) while((s32[]{:T(128)}, f32[8,128,128]{1,2,0:T(8,128)S(1)}, ...), condition=%wide.region_6.7_spmd, body=%wide.region_5.6_spmd.sunk | while | flops 403308544 | bytes 7340196 | solution.py:41
  203.8 1.1 constant_dynamic-slice_fusion.7
  207.5 1.1 constant_dynamic-slice_fusion.7
  211.3 1.1 constant_dynamic-slice_fusion.7
  (180 shorter events, 35.1 us)
Async XLA Ops:
  7.2 101.8 %copy-start = (bf16[128,512]{1,0:T(8,128)(2,1)S(1)}, bf16[128,512]{1,0:T(8,128)(2,1)}, u32[]{:S(2)}) copy-start(bf16[128,512]{1,0:T(8,128)(2,1)} %param.30) | copy-start | bytes 393220
  7.2 195.9 %all-gather.8.cloned.1.call-start = ((), (), s32[]{:S(2)}) async-start(), calls=%async_computation.1 | async-start | bytes 1310720 | tf_op jit(solution)/shard_map/all_gather | solution.py:25
  7.2 3.5 %copy-start.13 = (bf16[128,512]{1,0:T(8,128)(2,1)S(1)}, bf16[128,512]{1,0:T(8,128)(2,1)}, u32[]{:S(2)}) copy-start(bf16[128,512]{1,0:T(8,128)(2,1)} %param.21) | copy-start | bytes 393220
  9.0 1.3 copy-start.22
  11.3 1.0 copy-start.9
  97.3 0.9 copy-start.2
  97.3 105.8 %all-gather.6.cloned.1.call-start = ((), (), s32[]{:S(2)}) async-start(), calls=%async_computation | async-start | bytes 1310720 | tf_op jit(solution)/shard_map/all_gather | solution.py:25
  98.8 68.4 %collective-permute-start = (bf16[128,256]{1,0:T(8,128)(2,1)}, bf16[128,256]{1,0:T(8,128)(2,1)}, u32[]{:S(2)}, u32[]{:S(2)}) collective-permute-start(bf16[128,256]{1,0:T(8,128)(2,1)} %constant_dynamic-slice_fusion.2), channel_id=1, source_target_pairs={{0,4},{4,8},{8,12},{12,0},{1,5},{5,9},{9,13},{13,1},{2,6},{6,10},{... | collective-permute-start | bytes 196616 | tf_op jit(solution)/shard_map/ppermute | solution.py:272
  99.0 97.6 %collective-permute-start.2 = (bf16[128,256]{1,0:T(8,128)(2,1)}, bf16[128,256]{1,0:T(8,128)(2,1)}, u32[]{:S(2)}, u32[]{:S(2)}) collective-permute-start(bf16[128,256]{1,0:T(8,128)(2,1)} %constant_dynamic-slice_fusion.2), channel_id=1, source_target_pairs={{0,12},{4,0},{8,4},{12,8},{1,13},{5,1},{9,5},{13,9},{2,14},{6,2},{... | collective-permute-start | bytes 196616 | tf_op jit(solution)/shard_map/ppermute | solution.py:274
  102.7 0.9 copy-start.10
  104.1 0.9 copy-start.14
  126.1 0.9 copy-start.16
  127.0 35.5 %copy-start.6 = (pred[128,512]{1,0:T(8,128)(4,1)}, pred[128,512]{1,0:T(8,128)(4,1)S(1)}, u32[]{:S(2)}) copy-start(pred[128,512]{1,0:T(8,128)(4,1)S(1)} %fusion.50) | copy-start | bytes 196612
  127.0 15.6 %copy-start.24 = (s32[8]{0:T(128)S(1)}, s32[8]{0:T(128)}, u32[]{:S(2)}) copy-start(s32[8]{0:T(128)} %param.37) | copy-start | bytes 100
  127.0 16.1 %copy-start.17 = (bf16[2,64,512]{2,1,0:T(8,128)(2,1)S(1)}, bf16[2,64,512]{2,1,0:T(8,128)(2,1)}, u32[]{:S(2)}) copy-start(bf16[2,64,512]{2,1,0:T(8,128)(2,1)} %param.33) | copy-start | bytes 393220
  142.7 17.1 %copy-start.11 = (bf16[128,1024]{1,0:T(8,128)(2,1)S(1)}, bf16[128,1024]{1,0:T(8,128)(2,1)}, u32[]{:S(2)}) copy-start(bf16[128,1024]{1,0:T(8,128)(2,1)} %param.29) | copy-start | bytes 786436
  160.1 1.0 copy-start.12
  161.1 0.9 copy-start.5
  162.5 1.0 copy-start.4
  163.5 1.8 copy-start.15
  167.2 27.6 %collective-permute-start.1 = (bf16[128,256]{1,0:T(8,128)(2,1)}, bf16[128,256]{1,0:T(8,128)(2,1)}, u32[]{:S(2)}, u32[]{:S(2)}) collective-permute-start(bf16[128,256]{1,0:T(8,128)(2,1)} %collective-permute-done), channel_id=1, source_target_pairs={{0,4},{4,8},{8,12},{12,0},{1,5},{5,9},{9,13},{13,1},{2,6},{6,10},{... | collective-permute-start | bytes 196616 | tf_op jit(solution)/shard_map/ppermute | solution.py:272
  194.8 1.8 copy-start.3
  194.8 5.2 %copy-start.27 = (f32[128,4,256]{2,0,1:T(8,128)S(1)}, f32[128,4,256]{2,0,1:T(8,128)}, u32[]{:S(2)}) copy-start(f32[128,4,256]{2,0,1:T(8,128)} %fusion.18) | copy-start | bytes 1572868
  215.7 1.0 copy-start.1
  (9 other events, 6.4 us)
Sparse Core Ops, SparseCore 0:
  97.4 31.6 all-gather.7
  131.3 32.1 all-gather.5
